TPU v7x, 128 devices: a whole 4x4x4 slice. The times are simulated.
128 devices in a mesh: row: 8 (over z_hi, x), blk: 16 (over z_lo, y, core).
Axes of the slice: x: 4, y: 4, z: 4 (z_hi: 2, z_lo: 2; z = z_hi * 2 + z_lo), core: 2. Of those that a mesh axis runs over, the one named last changes fastest.
Arguments:
- spike_counts: int32 [16384, 2048], P(('row', 'blk')), may hold values from 0 to 23, as said below
- kernel_taps: int32 [16], replicated, may hold values from 1 to 8
- lag_bins: int32 [2], replicated, may hold values from 1 to 32, as said below
Outputs:
- correlogram: bfloat16 [2, 16384, 8, 2048], P(None, 'row', None, 'blk')
Inputs may be any that keep to these rules, and one draw needn't show every extreme that they name: `spike_counts`: neurons fire at different rates and share a common drive. `lag_bins`: the second lag equals 32; the first lies between 1 and 31.
All inputs are finite; a program needn't handle non-finite values.
Results may differ from a plain program's by a relative error of at most 0.0034.
Values may be sent and summed in bfloat16 or wider, within the bound.
A program may use at most 128 MiB of HBM per device.

v0:
```python
import jax
import jax.numpy as jnp
from jax import lax
from jax.sharding import PartitionSpec as P

NEURONS = 16384
BINS = 2048
TAPS = 16


def smoothed(spike_counts, kernel_taps):
    counts = spike_counts.astype(jnp.float32)
    weights = kernel_taps.astype(jnp.float32) / jnp.sum(kernel_taps.astype(jnp.float32))
    padded = jnp.pad(counts, ((0, 0), (TAPS - 1, 0)))
    result = jnp.zeros_like(counts)
    for delay in range(TAPS):
        result = result + weights[delay] * padded[:, TAPS - 1 - delay : TAPS - 1 - delay + BINS]
    return result


def later_bins(data, lag):
    padded = jnp.pad(data, ((0, 0), (0, BINS)))
    return lax.dynamic_slice_in_dim(padded, lag, BINS, 1)


def shards(spike_counts, kernel_taps, lag_bins):
    smooth = smoothed(spike_counts, kernel_taps)
    centred = smooth - jnp.mean(smooth, axis=1, keepdims=True)
    totals = lax.psum(jnp.sum(centred, axis=0), ("row", "blk"))
    residual_part = centred - (totals / NEURONS)[None, :]
    zscored = (
        residual_part
        * lax.rsqrt(jnp.mean(residual_part * residual_part, axis=1, keepdims=True) + 1e-05)
    ).astype(jnp.bfloat16)
    span_rows = zscored.shape[0]
    groups = lax.axis_size("row")
    columns = lax.all_gather(zscored, "row", axis=0, tiled=True)
    stacked = jnp.concatenate(
        [later_bins(columns, lag_bins[0]), later_bins(columns, lag_bins[1])], axis=0
    )
    piece = lax.all_gather(zscored, "blk", axis=0, tiled=True)
    product = jnp.dot(piece, stacked.T, preferred_element_type=jnp.float32) / BINS
    product = product.reshape(piece.shape[0], 2, groups, span_rows)
    return jnp.transpose(product, (1, 0, 2, 3)).astype(jnp.bfloat16)


def solution(mesh):
    placed = (P(("row", "blk"), None), P(), P())
    return jax.shard_map(
        shards, mesh=mesh, in_specs=placed, out_specs=P(None, "row", None, "blk"), check_vma=False
    )
```

profile of v0, /device:TPU:1, one launch (start us, length us, event | category | flops | bytes accessed | tf_op | source)
XLA Modules:
  0.0 258.9 jit_solution(15566849793997691235)
XLA Ops:
  6.5 0.0 copy-start
  6.5 0.0 all-gather.5.cloned.1.call-start
  6.5 1.3 convert_reduce_fusion
  7.8 1.3 convert_divide_fusion
  9.1 0.7 fusion.8
  9.8 1.3 convert_element_type.25
  11.2 14.1 %fusion.6 = (f32[128]{0:T(128)S(1)}, f32[128,2048]{1,0:T(8,128)S(1)}) fusion(f32[]{:T(128)} %bitcast.15, f32[]{:T(128)} %bitcast.14, f32[]{:T(128)} %bitcast.13, f32[]{:T(128)} %bitcast.12, f32[]{:T(128)} %bitcast.11, f32[]{:T(128)} %bitcast.10, f32[]{:T(128)} %bitcast.9, f32[]{:T(128)} %bitcast.8, f32[]{:T(128)} %bitcast.7, f32[]{:T(128)} %bitcast.6, ...), kind=kLoop, calls=%fused_computation.19 | loop fusion | flops 8388480 | bytes 2097728 | tf_op jit(solution)/shard_map/reduce_sum | solution.py:28
  25.3 0.2 subtract_reduce_fusion
  25.5 68.7 %psum.7 = f32[2048]{0:T(1024)S(1)} all-reduce(f32[2048]{0:T(1024)S(1)} %subtract_reduce_fusion), channel_id=1, replica_groups=mesh['row'=8,'blk'=16] {'row','blk'}, use_global_device_ids=true, to_apply=%region_3.4 | all-reduce | flops 2048 | bytes 16384 | tf_op jit(solution)/shard_map/psum | solution.py:29
  94.2 0.3 multiply_reduce_fusion
  94.5 1.0 multiply_convert_fusion.1
  95.5 0.0 all-gather.5.cloned.1.call-update
  95.6 0.2 all-gather.3.cloned.1.call-start
  95.8 0.5 all-gather.3.cloned.1.call-update
  96.3 0.0 copy-done
  96.3 0.6 fusion.7
  100.7 62.5 %all-gather.5.cloned.1.call-done = bf16[1024,2048]{1,0:T(8,128)(2,1)} async-done(((bf16[128,2048]{1,0:T(8,128)(2,1)}), bf16[1024,2048]{1,0:T(8,128)(2,1)}) %all-gather.5.cloned.1.call-update) | async-done | bytes 4194320 | tf_op jit(solution)/shard_map/all_gather | solution.py:37
  163.2 10.0 %pad_dynamic-slice_fusion.1 = (bf16[1024,2048]{1,0:T(8,128)(2,1)}, bf16[1024,2048]{1,0:T(8,128)(2,1)}) fusion(s32[]{:T(128)S(6)} %select_n.6, bf16[1024,2048]{1,0:T(8,128)(2,1)} %all-gather.5.cloned.1.call-done, s32[]{:T(128)S(6)} %select_n.7), kind=kLoop, calls=%fused_computation.2 | loop fusion | bytes 12582920 | tf_op jit(solution)/shard_map/dynamic_slice | solution.py:23
  173.2 42.5 %all-gather.3.cloned.1.call-done = bf16[2048,2048]{1,0:T(8,128)(2,1)} async-done(((bf16[128,2048]{1,0:T(8,128)(2,1)}), bf16[2048,2048]{1,0:T(8,128)(2,1)}) %all-gather.3.cloned.1.call-update) | async-done | bytes 8388624 | tf_op jit(solution)/shard_map/all_gather | solution.py:41
  215.7 23.8 %multiply_convert_fusion = bf16[2048,2048]{0,1:T(8,128)(2,1)} fusion(bf16[2048,2048]{1,0:T(8,128)(2,1)} %all-gather.3.cloned.1.call-done, bf16[1024,2048]{1,0:T(8,128)(2,1)} %get-tuple-element.8, bf16[1024,2048]{1,0:T(8,128)(2,1)} %get-tuple-element.7), kind=kOutput, calls=%fused_computation | convolution fusion | flops 17205035008 | bytes 25165824 | tf_op jit(solution)/shard_map/dot_general | solution.py:42
  239.5 12.6 %copy.4 = bf16[2048,2,8,128]{3,2,0,1:T(8,128)(2,1)} copy(bf16[2048,2,8,128]{0,3,2,1:T(8,128)(2,1)} %bitcast.21) | data formatting | bytes 16777216 | tf_op jit(solution)/shard_map/convert_element_type | solution.py:44
  (3 shorter events, 0.0 us)
Async XLA Ops:
  6.5 89.8 %copy-start = (s32[2]{0:T(128)S(1)}, s32[2]{0:T(128)}, u32[]{:S(2)}) copy-start(s32[2]{0:T(128)} %param.5) | copy-start | bytes 28
  6.5 156.7 %all-gather.5.cloned.1.call-start = ((), (), s32[]{:S(2)}) async-start(), calls=%async_computation.1 | async-start | bytes 4718592 | tf_op jit(solution)/shard_map/all_gather | solution.py:37
  95.6 120.2 %all-gather.3.cloned.1.call-start = ((), (), s32[]{:S(2)}) async-start(), calls=%async_computation | async-start | bytes 8912896 | tf_op jit(solution)/shard_map/all_gather | solution.py:41
Sparse Core Ops, SparseCore 0:
  95.7 67.5 all-gather.4
  165.0 50.7 all-gather.2
where the time goes:
time: 260 us; the launch traced here: 259 us
  waiting for transfers between devices  106 us (41%)
  blocking collectives  68.7 us (26%)
  local copies, waits for them, and re-layouts  23.9 us (9%)
  matrix products  23.8 us (9%)
  other arithmetic  19.5 us (8%)
  between operations  17.2 us (7%)
    psum x1, blocking collectives, shards(): totals = lax.psum(jnp.sum(centred, axis=0), ('row', 'blk'))  68.7 us
    all_gather x1, waiting for transfers between devices, shards(): columns = lax.all_gather(zscored, 'row', axis=0, tiled=True)  62.5 us
    all_gather x1, waiting for transfers between devices, shards(): piece = lax.all_gather(zscored, 'blk', axis=0, tiled=True)  42.5 us
    dot_general x1, matrix products, shards(): jnp.dot(piece, stacked.T, preferred_element_type=jnp.float32) / BINS  23.8 us
    reduce_sum x1, other arithmetic, shards(): centred = smooth - jnp.mean(smooth, axis=1, keepdims=True)  14.1 us
    convert_element_type x1, local copies, waits for them, and re-layouts, shards(): return jnp.transpose(product, (1, 0, 2, 3)).astype(jnp.bfloat16)  12.6 us
    dynamic_slice x1, local copies, waits for them, and re-layouts, later_bins(): return lax.dynamic_slice_in_dim(padded, lag, BINS, 1)  9.97 us
  transfers between devices with their start and end apart: 2, of which 2 were waited for; matrix products, arithmetic and copies ran while one was open for 4% of the time, Pallas kernels for 0%

commit v1 on v0

--- a/solution.py
+++ b/solution.py
@@ -26,7 +26,7 @@
 def shards(spike_counts, kernel_taps, lag_bins):
     smooth = smoothed(spike_counts, kernel_taps)
     centred = smooth - jnp.mean(smooth, axis=1, keepdims=True)
-    totals = lax.psum(jnp.sum(centred, axis=0), ("row", "blk"))
+    totals = lax.psum(lax.psum(jnp.sum(centred, axis=0), "blk"), "row")
     residual_part = centred - (totals / NEURONS)[None, :]
     zscored = (
         residual_part

time: 260 us -> 245 us (0.942)
  blocking collectives: 68.7 us -> 50.3 us
  waiting for transfers between devices: 106 us -> 109 us
    psum x1 -> x2, blocking collectives: 68.7 us -> 50.3 us  [shards(): totals = lax.psum(lax.psum(jnp.sum(centred, axis=0), 'blk'), 'row')]
    all_gather x1, waiting for transfers between devices: 62.5 us -> 66.5 us  [shards(): columns = lax.all_gather(zscored, 'row', axis=0, tiled=True)]
where the time goes in v1:
time: 245 us; the launch traced here: 244 us
  waiting for transfers between devices  109 us (44%)
  blocking collectives  50.3 us (21%)
  local copies, waits for them, and re-layouts  23.9 us (10%)
  matrix products  23.8 us (10%)
  other arithmetic  19.5 us (8%)
  between operations  17.2 us (7%)
    all_gather x1, waiting for transfers between devices, shards(): columns = lax.all_gather(zscored, 'row', axis=0, tiled=True)  66.5 us
    psum x2, blocking collectives, shards(): totals = lax.psum(lax.psum(jnp.sum(centred, axis=0), 'blk'), 'row')  50.3 us
    all_gather x1, waiting for transfers between devices, shards(): piece = lax.all_gather(zscored, 'blk', axis=0, tiled=True)  42.5 us
    dot_general x1, matrix products, shards(): jnp.dot(piece, stacked.T, preferred_element_type=jnp.float32) / BINS  23.8 us
    reduce_sum x1, other arithmetic, shards(): centred = smooth - jnp.mean(smooth, axis=1, keepdims=True)  14.1 us
    convert_element_type x1, local copies, waits for them, and re-layouts, shards(): return jnp.transpose(product, (1, 0, 2, 3)).astype(jnp.bfloat16)  12.6 us
    dynamic_slice x1, local copies, waits for them, and re-layouts, later_bins(): return lax.dynamic_slice_in_dim(padded, lag, BINS, 1)  9.97 us
  transfers between devices with their start and end apart: 2, of which 2 were waited for; matrix products, arithmetic and copies ran while one was open for 4% of the time, Pallas kernels for 0%

profile of v1, /device:TPU:1, one launch (start us, length us, event | category | flops | bytes accessed | tf_op | source)
XLA Modules:
  0.0 244.4 jit_solution(10958570971838929804)
XLA Ops:
  6.5 0.0 copy-start
  6.5 0.0 all-gather.5.cloned.1.call-start
  6.5 1.3 convert_reduce_fusion
  7.8 1.3 convert_divide_fusion
  9.1 0.7 fusion.8
  9.8 1.3 convert_element_type.25
  11.2 14.1 %fusion.6 = (f32[128]{0:T(128)S(1)}, f32[128,2048]{1,0:T(8,128)S(1)}) fusion(f32[]{:T(128)} %bitcast.15, f32[]{:T(128)} %bitcast.14, f32[]{:T(128)} %bitcast.13, f32[]{:T(128)} %bitcast.12, f32[]{:T(128)} %bitcast.11, f32[]{:T(128)} %bitcast.10, f32[]{:T(128)} %bitcast.9, f32[]{:T(128)} %bitcast.8, f32[]{:T(128)} %bitcast.7, f32[]{:T(128)} %bitcast.6, ...), kind=kLoop, calls=%fused_computation.19 | loop fusion | flops 8388480 | bytes 2097728 | tf_op jit(solution)/shard_map/reduce_sum | solution.py:28
  25.3 0.2 subtract_reduce_fusion
  25.5 29.1 %psum.14 = f32[2048]{0:T(1024)S(1)} all-reduce(f32[2048]{0:T(1024)S(1)} %subtract_reduce_fusion), channel_id=1, replica_groups=mesh['row'=8,'blk'=16] {'blk'}, use_global_device_ids=true, to_apply=%region_3.4 | all-reduce | flops 2048 | bytes 16384 | tf_op jit(solution)/shard_map/psum | solution.py:29
  54.6 21.2 %psum.15 = f32[2048]{0:T(1024)S(1)} all-reduce(f32[2048]{0:T(1024)S(1)} %psum.14), channel_id=1, replica_groups=mesh['row'=8,'blk'=16] {'row'}, use_global_device_ids=true, to_apply=%region_4.5 | all-reduce | flops 2048 | bytes 16384 | tf_op jit(solution)/shard_map/psum | solution.py:29
  75.8 0.3 multiply_reduce_fusion
  76.1 1.0 multiply_convert_fusion.1
  77.2 0.0 all-gather.5.cloned.1.call-update
  77.2 0.2 all-gather.3.cloned.1.call-start
  77.4 0.5 all-gather.3.cloned.1.call-update
  77.9 0.0 copy-done
  77.9 0.6 fusion.7
  82.3 66.5 %all-gather.5.cloned.1.call-done = bf16[1024,2048]{1,0:T(8,128)(2,1)} async-done(((bf16[128,2048]{1,0:T(8,128)(2,1)}), bf16[1024,2048]{1,0:T(8,128)(2,1)}) %all-gather.5.cloned.1.call-update) | async-done | bytes 4194320 | tf_op jit(solution)/shard_map/all_gather | solution.py:37
  148.8 10.0 %pad_dynamic-slice_fusion.1 = (bf16[1024,2048]{1,0:T(8,128)(2,1)}, bf16[1024,2048]{1,0:T(8,128)(2,1)}) fusion(s32[]{:T(128)S(6)} %select_n.6, bf16[1024,2048]{1,0:T(8,128)(2,1)} %all-gather.5.cloned.1.call-done, s32[]{:T(128)S(6)} %select_n.7), kind=kLoop, calls=%fused_computation.2 | loop fusion | bytes 12582920 | tf_op jit(solution)/shard_map/dynamic_slice | solution.py:23
  158.8 42.5 %all-gather.3.cloned.1.call-done = bf16[2048,2048]{1,0:T(8,128)(2,1)} async-done(((bf16[128,2048]{1,0:T(8,128)(2,1)}), bf16[2048,2048]{1,0:T(8,128)(2,1)}) %all-gather.3.cloned.1.call-update) | async-done | bytes 8388624 | tf_op jit(solution)/shard_map/all_gather | solution.py:41
  201.2 23.8 %multiply_convert_fusion = bf16[2048,2048]{0,1:T(8,128)(2,1)} fusion(bf16[2048,2048]{1,0:T(8,128)(2,1)} %all-gather.3.cloned.1.call-done, bf16[1024,2048]{1,0:T(8,128)(2,1)} %get-tuple-element.8, bf16[1024,2048]{1,0:T(8,128)(2,1)} %get-tuple-element.7), kind=kOutput, calls=%fused_computation | convolution fusion | flops 17205035008 | bytes 25165824 | tf_op jit(solution)/shard_map/dot_general | solution.py:42
  225.0 12.6 %copy.4 = bf16[2048,2,8,128]{3,2,0,1:T(8,128)(2,1)} copy(bf16[2048,2,8,128]{0,3,2,1:T(8,128)(2,1)} %bitcast.21) | data formatting | bytes 16777216 | tf_op jit(solution)/shard_map/convert_element_type | solution.py:44
  (3 shorter events, 0.0 us)
Async XLA Ops:
  6.5 71.4 %copy-start = (s32[2]{0:T(128)S(1)}, s32[2]{0:T(128)}, u32[]{:S(2)}) copy-start(s32[2]{0:T(128)} %param.5) | copy-start | bytes 28
  6.5 142.3 %all-gather.5.cloned.1.call-start = ((), (), s32[]{:S(2)}) async-start(), calls=%async_computation.1 | async-start | bytes 4718592 | tf_op jit(solution)/shard_map/all_gather | solution.py:37
  77.2 124.1 %all-gather.3.cloned.1.call-start = ((), (), s32[]{:S(2)}) async-start(), calls=%async_computation | async-start | bytes 8912896 | tf_op jit(solution)/shard_map/all_gather | solution.py:41
Sparse Core Ops, SparseCore 0:
  77.3 71.4 all-gather.4
  150.5 50.7 all-gather.2
